TPU v7x, 32 devices: a whole 2x2x4 slice. The times are simulated.
32 devices in a mesh: lat: 8 (over z, y), lon: 4 (over x, core).
Axes of the slice: x: 2, y: 2, z: 4, core: 2. Of those that a mesh axis runs over, the one named last changes fastest.
Arguments:
- grid_fields: bfloat16 [1280, 50, 3, 2560], P('lat', None, None, 'lon'), may hold values from -6 to 6
- legendre: bfloat16 [512, 1280, 640], P(('lat', 'lon')), may hold values from -0.15625 to 0.15625
- wave_of_slot: int32 [512], replicated, may hold values from 0 to 511, as said below
- energy_weight: float32 [3, 640], replicated, may hold values from 0.1 to 10
Outputs:
- spectral: bfloat16 [50, 3, 512, 2, 640], P(None, None, ('lat', 'lon'))
- gram_matrix: float32 [50, 50], replicated
Inputs may be any that keep to these rules, and one draw needn't show every extreme that they name: `wave_of_slot`: every wavenumber 0 to 511 stands in exactly one slot; slot d * 16 + r holds a wavenumber of r * 32 to r * 32 + 31.
All inputs are finite; a program needn't handle non-finite values.
Results may differ from a plain program's by a relative error of at most 0.0043.
Values may be sent and summed in bfloat16 or wider, within the bound.
No kernel may reach another device: no remote copies, remote signals or barrier semaphores. Data moves between devices by JAX's collectives and lax.ppermute only.
A program may use at most 256 MiB of HBM per device.

v0:
```python
import math
import jax
import jax.numpy as jnp
from jax import lax
from jax.sharding import PartitionSpec as P

M = 512
NT = 640
LEV = 3


def make_trig(wave_list, lon_total):
    longitude = jnp.arange(lon_total, dtype=jnp.int32)
    phase_index = longitude[:, None] * wave_list[None, :] % lon_total
    angles = phase_index.astype(jnp.float32) * (2.0 * math.pi / lon_total)
    stacked = jnp.stack([jnp.cos(angles), -jnp.sin(angles)], axis=2)
    return stacked.reshape(lon_total, 2 * wave_list.shape[0]).astype(jnp.bfloat16)


def on_device(grid_fields, legendre, wave_of_slot, energy_weight):
    lat_dev, vectors, levels, lon_dev = grid_fields.shape
    bands = lax.axis_size("lat")
    sectors = lax.axis_size("lon")
    lon_total = lon_dev * sectors
    per_dev = legendre.shape[0]
    degrees = legendre.shape[2]
    fields = vectors * levels
    band_rows = lat_dev // sectors
    norm_scale = 1.0 / math.sqrt(lon_total)
    trig_table = make_trig(wave_of_slot, lon_total)
    moved_rows = lax.all_to_all(grid_fields, "lon", split_axis=0, concat_axis=3, tiled=True)
    product = jnp.dot(
        moved_rows.reshape(-1, lon_total), trig_table, preferred_element_type=jnp.float32
    )
    fourier = product.reshape(band_rows, fields, -1) * norm_scale
    gathered = lax.all_to_all(
        lax.all_to_all(fourier, "lat", split_axis=2, concat_axis=0, tiled=True),
        "lon",
        split_axis=2,
        concat_axis=0,
        tiled=True,
    )
    cols_here = gathered.shape[2]
    columns = gathered.reshape(sectors, bands, band_rows, fields, cols_here).transpose(
        1, 0, 2, 3, 4
    )
    columns = columns.reshape(bands * lat_dev, fields, cols_here)
    columns = columns.reshape(bands * lat_dev, fields, per_dev, 2)
    device_slot = (lax.axis_index("lat") * sectors + lax.axis_index("lon")) * per_dev
    own_waves = lax.dynamic_slice_in_dim(wave_of_slot, device_slot, per_dev, 0)
    degree_index = jnp.arange(degrees, dtype=jnp.int32)
    tri_mask = (degree_index[None, :] >= own_waves[:, None]).astype(jnp.float32)
    legendre_table = legendre.astype(jnp.float32) * tri_mask[:, None, :]
    spectral = jnp.einsum(
        "aftp,tan->ftpn", columns, legendre_table, precision=lax.Precision.HIGHEST
    )
    spectral = spectral.reshape(vectors, levels, per_dev, 2, degrees)
    factor = jnp.where(own_waves == 0, 1.0, 2.0).astype(jnp.float32)
    weighted = spectral * factor[None, None, :, None, None] * energy_weight[None, :, None, None, :]
    partial_value = jnp.dot(
        spectral.reshape(vectors, -1),
        weighted.reshape(vectors, -1).T,
        precision=lax.Precision.HIGHEST,
    )
    gram_matrix = lax.psum(partial_value, ("lat", "lon")) / (LEV * M * NT)
    return (spectral.astype(jnp.bfloat16), gram_matrix)


def solution(mesh):
    placed = (P("lat", None, None, "lon"), P(("lat", "lon"), None, None), P(), P())
    return jax.shard_map(
        on_device,
        mesh=mesh,
        in_specs=placed,
        out_specs=(P(None, None, ("lat", "lon"), None, None), P()),
        check_vma=False,
    )
```

profile of v0, /device:TPU:0, one launch (start us, length us, event | category | flops | bytes accessed | tf_op | source)
XLA Modules:
  0.0 2192.7 jit_solution(3052948345299898282)
XLA Ops:
  0.6 22.1 %copy.47 = bf16[160,50,3,640]{3,1,2,0:T(8,128)(2,1)} copy(bf16[160,50,3,640]{3,0,2,1:T(8,128)(2,1)} %param.4) | data formatting | bytes 61440000 | tf_op args[0]
  22.7 10.0 all-to-all-start
  32.8 22.3 %cosine_convert_fusion = (bf16[2560,512,1]{1,0,2:T(8,128)(2,1)S(1)}, bf16[2560,512,1]{1,0,2:T(8,128)(2,1)S(1)}) fusion(s32[512]{0:T(512)S(1)} %copy-done.1), kind=kLoop, calls=%fused_computation.14 | loop fusion | flops 15728640 | bytes 5244928 | tf_op jit(solution)/shard_map/convert
  55.0 2.8 pad_maximum_fusion
  57.9 13.9 copy.46
  71.8 11.6 convert_element_type.43
  83.4 321.9 %all-to-all-done = bf16[160,50,3,640]{3,1,2,0:T(8,128)(2,1)} async-done(((bf16[160,50,3,640]{3,1,2,0:T(8,128)(2,1)}), bf16[160,50,3,640]{3,1,2,0:T(8,128)(2,1)}, u32[]{:S(2)}, u32[]{:S(2)}) %all-to-all-start) | async-done | bytes 30720032 | tf_op jit(solution)/shard_map/all_to_all | solution.py:31
  405.4 27.3 %copy.48 = bf16[4,40,50,3,640]{4,0,3,2,1:T(4,128)(2,1)} copy(bf16[4,40,50,3,640]{4,2,3,1,0:T(8,128)(2,1)} %bitcast.2) | data formatting | bytes 61440000 | tf_op jit(solution)/shard_map/all_to_all | solution.py:31
  432.6 21.6 copy.67
  454.2 39.4 %multiply_bitcast_fusion = f32[6000,1024]{1,0:T(8,128)} fusion(bf16[2560,1024]{0,1:T(8,128)(2,1)} %convert_element_type.43, bf16[6000,2560]{1,0:T(8,128)(2,1)} %bitcast.48), kind=kOutput, calls=%fused_computation.5 | convolution fusion | flops 31463424000 | bytes 60538880 | tf_op jit(solution)/shard_map/dot_general | solution.py:32
  493.6 19.6 mul.105
  513.3 43.6 %copy.49 = f32[40,150,1024]{1,0,2:T(8,128)} copy(f32[40,150,1024]{2,1,0:T(8,128)} %mul.105) | data formatting | bytes 49152000 | tf_op jit(solution)/shard_map/mul | solution.py:35
  556.9 915.7 %all_to_all.48 = f32[40,150,1024]{1,0,2:T(8,128)} all-to-all(f32[40,150,1024]{1,0,2:T(8,128)} %copy.49), channel_id=1, replica_groups=mesh['lat'=8,'lon'=4] {'lat'}, dimensions={2} | all-to-all | bytes 49152000 | tf_op jit(solution)/shard_map/all_to_all | solution.py:37
  1472.6 36.6 %copy.51 = f32[8,40,150,128]{3,1,0,2:T(8,128)} copy(f32[8,40,150,128]{2,1,3,0:T(8,128)} %bitcast.44) | data formatting | bytes 49152000 | tf_op jit(solution)/shard_map/all_to_all | solution.py:37
  1509.2 28.0 %copy.52 = f32[320,150,128]{0,1,2:T(8,128)} copy(f32[320,150,128]{2,0,1:T(8,128)} %bitcast.47) | data formatting | bytes 49152000 | tf_op jit(solution)/shard_map/all_to_all | solution.py:37
  1537.2 9.6 all-to-all-start.2
  1546.9 0.2 mul.109
  1547.1 0.8 compare_select_fusion
  1548.0 322.3 %all-to-all-done.2 = f32[320,150,128]{0,1,2:T(8,128)} async-done(((f32[320,150,128]{0,1,2:T(8,128)}), f32[320,150,128]{0,1,2:T(8,128)}, u32[]{:S(2)}, u32[]{:S(2)}) %all-to-all-start.2) | async-done | bytes 24576032 | tf_op jit(solution)/shard_map/all_to_all | solution.py:36
  1870.3 46.2 %copy.54 = f32[4,320,150,32]{2,3,1,0:T(8,128)} copy(f32[4,320,150,32]{1,2,3,0:T(8,128)} %bitcast.11) | data formatting | bytes 49152000 | tf_op jit(solution)/shard_map/all_to_all | solution.py:36
  1916.5 39.3 %copy.55 = f32[8,4,40,150,32]{3,2,1,0,4:T(8,128)} copy(f32[8,4,40,150,32]{3,4,2,0,1:T(8,128)} %bitcast.45) | data formatting | bytes 49152000 | tf_op jit(solution)/shard_map/transpose | solution.py:44
  1955.7 76.5 %fusion = f32[16,640,150,2]{1,2,3,0:T(8,128)} fusion(f32[1280,150,16,2]{1,0,3,2:T(8,128)} %bitcast.43, bf16[16,1280,640]{2,1,0:T(8,128)(2,1)} %param.5, f32[16,640]{1,0:T(8,128)S(1)} %fusion.11), kind=kOutput, calls=%fused_computation | convolution fusion | flops 47212134400 | bytes 63119360 | tf_op jit(solution)/shard_map/aftp,tan->ftpn/dot_general | solution.py:54
  2032.2 8.0 copy.70
  2040.3 11.4 copy.60
  2051.6 22.5 %copy.58 = f32[150,16,2,640]{3,2,1,0:T(2,128)} copy(f32[150,16,2,640]{3,0,2,1:T(8,128)} %bitcast.42) | data formatting | bytes 24576000 | tf_op jit(solution)/shard_map/aftp,tan->ftpn/transpose | solution.py:54
  2074.1 15.4 reshape_reshape.7
  2089.5 13.2 fusion.5
  2102.6 18.4 copy.59
  2121.0 15.1 mul.112
  2136.1 16.4 fusion.12
  2152.5 39.1 %psum.7 = f32[50,50]{1,0:T(8,128)S(1)} all-reduce(f32[50,50]{1,0:T(8,128)S(1)} %fusion.12), channel_id=1, replica_groups=mesh['lat'=8,'lon'=4] {'lat','lon'}, use_global_device_ids=true, to_apply=%region_0.1 | all-reduce | flops 2500 | bytes 20000 | tf_op jit(solution)/shard_map/psum | solution.py:65
  2191.6 0.6 broadcast_multiply_fusion
  (6 shorter events, 0.1 us)
Async XLA Ops:
  22.7 10.0 copy-start.1
  22.7 382.6 %all-to-all-start = ((bf16[160,50,3,640]{3,1,2,0:T(8,128)(2,1)}), bf16[160,50,3,640]{3,1,2,0:T(8,128)(2,1)}, u32[]{:S(2)}, u32[]{:S(2)}) async-start(bf16[160,50,3,640]{3,1,2,0:T(8,128)(2,1)} %copy.47), calls=%async_computation | async-start | bytes 68812800 | tf_op jit(solution)/shard_map/all_to_all | solution.py:31
  1537.2 9.7 copy-start
  1537.2 333.1 %all-to-all-start.2 = ((f32[320,150,128]{0,1,2:T(8,128)}), f32[320,150,128]{0,1,2:T(8,128)}, u32[]{:S(2)}, u32[]{:S(2)}) async-start(f32[320,150,128]{0,1,2:T(8,128)} %copy.52), calls=%async_computation.2 | async-start | bytes 59768832 | tf_op jit(solution)/shard_map/all_to_all | solution.py:36
where the time goes:
time: 2210 us; the launch traced here: 2190 us
  blocking collectives  955 us (43%)
  waiting for transfers between devices  644 us (29%)
  local copies, waits for them, and re-layouts  401 us (18%)
  matrix products  132 us (6%)
  other arithmetic  39.7 us (2%)
    all_to_all x1, blocking collectives, on_device(): lax.all_to_all(fourier, 'lat', split_axis=2, concat_axis=0, tiled=True)  916 us
    all_to_all x1, waiting for transfers between devices, on_device(): lax.all_to_all(lax.all_to_all(fourier, 'lat', split_axis=2, concat_axis=0...  322 us
    all_to_all x1, waiting for transfers between devices, on_device(): lax.all_to_all(grid_fields, 'lon', split_axis=0, concat_axis=3, tiled=True)  322 us
    dot_general x1, matrix products, on_device(): jnp.einsum('aftp,tan->ftpn', columns, legendre_table, precision=lax.Preci...  76.5 us
    all_to_all x2, local copies, waits for them, and re-layouts, on_device(): lax.all_to_all(fourier, 'lat', split_axis=2, concat_axis=0, tiled=True)  64.6 us
    mul x2, local copies, waits for them, and re-layouts, on_device(): fourier = product.reshape(band_rows, fields, -1) * norm_scale  63.2 us
    unnamed x7, local copies, waits for them, and re-layouts  55 us
    all_to_all x1, local copies, waits for them, and re-layouts, on_device(): lax.all_to_all(lax.all_to_all(fourier, 'lat', split_axis=2, concat_axis=0...  46.2 us
  transfers between devices with their start and end apart: 2, of which 2 were waited for; matrix products, arithmetic and copies ran while one was open for 2% of the time, Pallas kernels for 0%

commit v1 on v0

--- a/solution.py
+++ b/solution.py
@@ -7,6 +7,22 @@
 M = 512
 NT = 640
 LEV = 3
+
+
+def swapped_with_each(x, axis, split, join):
+    ways, here = (lax.axis_size(axis), lax.axis_index(axis))
+    width = x.shape[split] // ways
+    lengths = list(x.shape)
+    lengths[split] = width
+    height = lengths[join]
+    lengths[join] = height * ways
+    full = jnp.zeros(lengths, x.dtype)
+    for mask in range(ways):
+        part = lax.dynamic_slice_in_dim(x, (here ^ mask) * width, width, axis=split)
+        if mask:
+            part = lax.ppermute(part, axis, [(d, d ^ mask) for d in range(ways)])
+        full = lax.dynamic_update_slice_in_dim(full, part, (here ^ mask) * height, axis=join)
+    return full
 
 
 def make_trig(wave_list, lon_total):
@@ -34,11 +50,7 @@
     )
     fourier = product.reshape(band_rows, fields, -1) * norm_scale
     gathered = lax.all_to_all(
-        lax.all_to_all(fourier, "lat", split_axis=2, concat_axis=0, tiled=True),
-        "lon",
-        split_axis=2,
-        concat_axis=0,
-        tiled=True,
+        swapped_with_each(fourier, "lat", 2, 0), "lon", split_axis=2, concat_axis=0, tiled=True
     )
     cols_here = gathered.shape[2]
     columns = gathered.reshape(sectors, bands, band_rows, fields, cols_here).transpose(

time: 2210 us -> 1940 us (0.88)
  blocking collectives: 955 us -> 39 us
  local copies, waits for them, and re-layouts: 401 us -> 853 us
  waiting for transfers between devices: 644 us -> 820 us
    all_to_all x1 -> x0, blocking collectives: 916 us -> none  [on_device(): lax.all_to_all(fourier, 'lat', split_axis=2, concat_axis=0, tiled=True)]
    dynamic_update_slice x0 -> x8, local copies, waits for them, and re-layouts: none -> 438 us  [swapped_with_each(): lax.dynamic_update_slice_in_dim(full, part, (here ^ mask) * height, axis=...]
    ppermute x0 -> x7, waiting for transfers between devices: none -> 176 us  [swapped_with_each(): part = lax.ppermute(part, axis, [(d, d ^ mask) for d in range(ways)])]
    ppermute x0 -> x7, local copies, waits for them, and re-layouts: none -> 69.2 us  [swapped_with_each(): part = lax.ppermute(part, axis, [(d, d ^ mask) for d in range(ways)])]
    all_to_all x3 -> x1, local copies, waits for them, and re-layouts: 111 us -> 46.2 us  [on_device(): lax.all_to_all(swapped_with_each(fourier, 'lat', 2, 0), 'lon', split_axis...]
    mul x2 -> x1, local copies, waits for them, and re-layouts: 63.2 us -> 19.7 us  [on_device(): fourier = product.reshape(band_rows, fields, -1) * norm_scale]
    dynamic_slice x0 -> x9, local copies, waits for them, and re-layouts: none -> 39.1 us  [swapped_with_each(): part = lax.dynamic_slice_in_dim(x, (here ^ mask) * width, width, axis=split)]
    unnamed x7 -> x25, local copies, waits for them, and re-layouts: 55 us -> 55.4 us
  transfers between devices with their start and end apart: 2 -> 9, of which waited for: 2 -> 4; matrix products, arithmetic and copies ran while one was open for 2% -> 27% of each run, Pallas kernels for 0% -> 0%
where the time goes in v1:
time: 1940 us; the launch traced here: 1920 us
  local copies, waits for them, and re-layouts  853 us (44%)
  waiting for transfers between devices  820 us (42%)
  matrix products  133 us (7%)
  other arithmetic  39.6 us (2%)
  blocking collectives  39 us (2%)
  starting transfers between devices  31.7 us (2%)
    dynamic_update_slice x8, local copies, waits for them, and re-layouts, swapped_with_each(): lax.dynamic_update_slice_in_dim(full, part, (here ^ mask) * height, axis=...  438 us
    all_to_all x1, waiting for transfers between devices, on_device(): lax.all_to_all(swapped_with_each(fourier, 'lat', 2, 0), 'lon', split_axis...  322 us
    all_to_all x1, waiting for transfers between devices, on_device(): lax.all_to_all(grid_fields, 'lon', split_axis=0, concat_axis=3, tiled=True)  322 us
    ppermute x7, waiting for transfers between devices, swapped_with_each(): part = lax.ppermute(part, axis, [(d, d ^ mask) for d in range(ways)])  176 us
    dot_general x1, matrix products, on_device(): jnp.einsum('aftp,tan->ftpn', columns, legendre_table, precision=lax.Preci...  77 us
    ppermute x7, local copies, waits for them, and re-layouts, swapped_with_each(): part = lax.ppermute(part, axis, [(d, d ^ mask) for d in range(ways)])  69.2 us
    unnamed x25, local copies, waits for them, and re-layouts  55.4 us
    all_to_all x1, local copies, waits for them, and re-layouts, on_device(): lax.all_to_all(swapped_with_each(fourier, 'lat', 2, 0), 'lon', split_axis...  46.2 us
  transfers between devices with their start and end apart: 9, of which 4 were waited for; matrix products, arithmetic and copies ran while one was open for 27% of the time, Pallas kernels for 0%

profile of v1, /device:TPU:0, one launch (start us, length us, event | category | flops | bytes accessed | tf_op | source)
XLA Modules:
  0.0 1917.0 jit_solution(2389438935901089704)
XLA Ops:
  0.6 22.1 %copy.74 = bf16[160,50,3,640]{3,1,2,0:T(8,128)(2,1)} copy(bf16[160,50,3,640]{3,0,2,1:T(8,128)(2,1)} %param.4) | data formatting | bytes 61440000 | tf_op args[0]
  32.8 22.3 %cosine_convert_fusion = (bf16[2560,512,1]{1,0,2:T(8,128)(2,1)S(1)}, bf16[2560,512,1]{1,0,2:T(8,128)(2,1)S(1)}) fusion(s32[512]{0:T(512)S(1)} %copy-done.10), kind=kLoop, calls=%fused_computation.14 | loop fusion | flops 15728640 | bytes 5244928 | tf_op jit(solution)/shard_map/convert
  57.9 13.9 copy.73
  71.8 11.6 convert_element_type.43
  83.4 321.9 %all-to-all-done = bf16[160,50,3,640]{3,1,2,0:T(8,128)(2,1)} async-done(((bf16[160,50,3,640]{3,1,2,0:T(8,128)(2,1)}), bf16[160,50,3,640]{3,1,2,0:T(8,128)(2,1)}, u32[]{:S(2)}, u32[]{:S(2)}) %all-to-all-start) | async-done | bytes 30720032 | tf_op jit(solution)/shard_map/all_to_all | solution.py:47
  405.3 27.3 %copy.75 = bf16[4,40,50,3,640]{4,0,3,2,1:T(4,128)(2,1)} copy(bf16[4,40,50,3,640]{4,2,3,1,0:T(8,128)(2,1)} %bitcast.2) | data formatting | bytes 61440000 | tf_op jit(solution)/shard_map/all_to_all | solution.py:47
  432.6 21.5 %copy.103 = bf16[750,8,4,640]{3,1,2,0:T(8,128)(2,1)} copy(bf16[750,8,4,640]{3,2,1,0:T(4,128)(2,1)} %bitcast.40) | data formatting | bytes 61440000
  454.1 39.5 %multiply_bitcast_fusion = f32[6000,1024]{1,0:T(8,128)} fusion(bf16[2560,1024]{0,1:T(8,128)(2,1)} %convert_element_type.43, bf16[6000,2560]{1,0:T(8,128)(2,1)} %bitcast.41), kind=kOutput, calls=%fused_computation.5 | convolution fusion | flops 31463424000 | bytes 60538880 | tf_op jit(solution)/shard_map/dot_general | solution.py:48
  493.6 19.7 %mul.153 = f32[40,150,1024]{2,1,0:T(8,128)} reshape(f32[6000,1024]{1,0:T(8,128)} %multiply_bitcast_fusion) | data formatting | bytes 49152000 | tf_op jit(solution)/shard_map/mul | solution.py:51
  513.2 15.8 constant_dynamic-slice_fusion
  549.4 50.9 %collective-permute-done = f32[40,150,128]{2,0,1:T(8,128)S(1)} collective-permute-done((f32[40,150,128]{2,0,1:T(8,128)S(1)}, f32[40,150,128]{2,0,1:T(8,128)S(1)}, u32[]{:S(2)}, u32[]{:S(2)}) %collective-permute-start) | collective-permute-done | bytes 3072032 | tf_op jit(solution)/shard_map/ppermute | solution.py:23
  606.4 124.6 %collective-permute-done.1 = f32[40,150,128]{2,0,1:T(8,128)S(1)} collective-permute-done((f32[40,150,128]{2,0,1:T(8,128)S(1)}, f32[40,150,128]{2,0,1:T(8,128)S(1)}, u32[]{:S(2)}, u32[]{:S(2)}) %collective-permute-start.1) | collective-permute-done | bytes 3072032 | tf_op jit(solution)/shard_map/ppermute | solution.py:23
  741.9 11.8 broadcast_in_dim.10
  753.7 43.1 %dynamic_update_slice.24 = f32[320,150,128]{0,1,2:T(8,128)} dynamic-update-slice(f32[320,150,128]{0,1,2:T(8,128)} %broadcast_in_dim.10, f32[40,150,128]{0,1,2:T(8,128)} %copy.76, s32[]{:T(128)S(6)} %select_n.76, s32[]{:T(128)} %constant.11.clone.1, s32[]{:T(128)} %constant.11.clone.1) | dynamic-update-slice | bytes 6144004 | tf_op jit(solution)/shard_map/dynamic_update_slice | solution.py:24
  806.6 56.8 %dynamic_update_slice.25 = f32[320,150,128]{0,1,2:T(8,128)} dynamic-update-slice(f32[320,150,128]{0,1,2:T(8,128)} %dynamic_update_slice.24, f32[40,150,128]{0,1,2:T(8,128)} %copy.78, s32[]{:T(128)S(6)} %select_n.78, s32[]{:T(128)} %constant.11.clone.1, s32[]{:T(128)} %constant.11.clone.1) | dynamic-update-slice | bytes 6144004 | tf_op jit(solution)/shard_map/dynamic_update_slice | solution.py:24
  873.2 56.6 %dynamic_update_slice.26 = f32[320,150,128]{0,1,2:T(8,128)} dynamic-update-slice(f32[320,150,128]{0,1,2:T(8,128)} %dynamic_update_slice.25, f32[40,150,128]{0,1,2:T(8,128)} %copy.80, s32[]{:T(128)S(6)} %select_n.80, s32[]{:T(128)} %constant.11.clone.1, s32[]{:T(128)} %constant.11.clone.1) | dynamic-update-slice | bytes 6144004 | tf_op jit(solution)/shard_map/dynamic_update_slice | solution.py:24
  939.9 56.6 %dynamic_update_slice.27 = f32[320,150,128]{0,1,2:T(8,128)} dynamic-update-slice(f32[320,150,128]{0,1,2:T(8,128)} %dynamic_update_slice.26, f32[40,150,128]{0,1,2:T(8,128)} %copy.82, s32[]{:T(128)S(6)} %select_n.82, s32[]{:T(128)} %constant.11.clone.1, s32[]{:T(128)} %constant.11.clone.1) | dynamic-update-slice | bytes 6144004 | tf_op jit(solution)/shard_map/dynamic_update_slice | solution.py:24
  1006.4 56.6 %dynamic_update_slice.28 = f32[320,150,128]{0,1,2:T(8,128)} dynamic-update-slice(f32[320,150,128]{0,1,2:T(8,128)} %dynamic_update_slice.27, f32[40,150,128]{0,1,2:T(8,128)} %copy.84, s32[]{:T(128)S(6)} %select_n.84, s32[]{:T(128)} %constant.11.clone.1, s32[]{:T(128)} %constant.11.clone.1) | dynamic-update-slice | bytes 6144004 | tf_op jit(solution)/shard_map/dynamic_update_slice | solution.py:24
  1072.9 56.6 %dynamic_update_slice.29 = f32[320,150,128]{0,1,2:T(8,128)} dynamic-update-slice(f32[320,150,128]{0,1,2:T(8,128)} %dynamic_update_slice.28, f32[40,150,128]{0,1,2:T(8,128)} %copy.86, s32[]{:T(128)S(6)} %select_n.86, s32[]{:T(128)} %constant.11.clone.1, s32[]{:T(128)} %constant.11.clone.1) | dynamic-update-slice | bytes 6144004 | tf_op jit(solution)/shard_map/dynamic_update_slice | solution.py:24
  1139.4 56.6 %dynamic_update_slice.30 = f32[320,150,128]{0,1,2:T(8,128)} dynamic-update-slice(f32[320,150,128]{0,1,2:T(8,128)} %dynamic_update_slice.29, f32[40,150,128]{0,1,2:T(8,128)} %copy.88, s32[]{:T(128)S(6)} %select_n.88, s32[]{:T(128)} %constant.11.clone.1, s32[]{:T(128)} %constant.11.clone.1) | dynamic-update-slice | bytes 6144004 | tf_op jit(solution)/shard_map/dynamic_update_slice | solution.py:24
  1205.9 55.0 %dynamic_update_slice.31 = f32[320,150,128]{0,1,2:T(8,128)} dynamic-update-slice(f32[320,150,128]{0,1,2:T(8,128)} %dynamic_update_slice.30, f32[40,150,128]{0,1,2:T(8,128)} %copy.90, s32[]{:T(128)S(6)} %select_n.90, s32[]{:T(128)} %constant.11.clone.1, s32[]{:T(128)} %constant.11.clone.1) | dynamic-update-slice | bytes 6144004 | tf_op jit(solution)/shard_map/dynamic_update_slice | solution.py:24
  1271.4 322.3 %all-to-all-done.1 = f32[320,150,128]{0,1,2:T(8,128)} async-done(((f32[320,150,128]{0,1,2:T(8,128)}), f32[320,150,128]{0,1,2:T(8,128)}, u32[]{:S(2)}, u32[]{:S(2)}) %all-to-all-start.1) | async-done | bytes 24576032 | tf_op jit(solution)/shard_map/all_to_all | solution.py:52
  1593.7 46.2 %copy.92 = f32[4,320,150,32]{2,3,1,0:T(8,128)} copy(f32[4,320,150,32]{1,2,3,0:T(8,128)} %bitcast.7) | data formatting | bytes 49152000 | tf_op jit(solution)/shard_map/all_to_all | solution.py:52
  1639.9 39.1 %copy.93 = f32[8,4,40,150,32]{3,2,1,0,4:T(8,128)} copy(f32[8,4,40,150,32]{3,4,2,0,1:T(8,128)} %bitcast.39) | data formatting | bytes 49152000 | tf_op jit(solution)/shard_map/transpose | solution.py:56
  1679.0 77.0 %fusion = f32[16,640,150,2]{1,2,3,0:T(8,128)} fusion(f32[1280,150,16,2]{1,0,3,2:T(8,128)} %bitcast.38, bf16[16,1280,640]{2,1,0:T(8,128)(2,1)} %param.5, f32[16,640]{1,0:T(8,128)S(1)} %fusion.11), kind=kOutput, calls=%fused_computation | convolution fusion | flops 47212134400 | bytes 63119360 | tf_op jit(solution)/shard_map/aftp,tan->ftpn/dot_general | solution.py:66
  1766.6 13.1 fusion.5
  1779.7 18.4 copy.97
  1798.1 15.1 mul.176
  1813.2 22.6 %copy.96 = f32[150,16,2,640]{3,2,1,0:T(2,128)} copy(f32[150,16,2,640]{3,0,2,1:T(8,128)} %bitcast.37) | data formatting | bytes 24576000 | tf_op jit(solution)/shard_map/aftp,tan->ftpn/transpose | solution.py:66
  1835.8 15.1 reshape_reshape.7
  1850.9 16.2 fusion.12
  1867.1 39.0 %psum.7 = f32[50,50]{1,0:T(8,128)S(1)} all-reduce(f32[50,50]{1,0:T(8,128)S(1)} %fusion.12), channel_id=1, replica_groups=mesh['lat'=8,'lon'=4] {'lat','lon'}, use_global_device_ids=true, to_apply=%region_0.1 | all-reduce | flops 2500 | bytes 20000 | tf_op jit(solution)/shard_map/psum | solution.py:77
  (59 shorter events, 151.1 us)
Async XLA Ops:
  22.7 10.1 copy-start.10
  22.7 382.6 %all-to-all-start = ((bf16[160,50,3,640]{3,1,2,0:T(8,128)(2,1)}), bf16[160,50,3,640]{3,1,2,0:T(8,128)(2,1)}, u32[]{:S(2)}, u32[]{:S(2)}) async-start(bf16[160,50,3,640]{3,1,2,0:T(8,128)(2,1)} %copy.74), calls=%async_computation | async-start | bytes 68812800 | tf_op jit(solution)/shard_map/all_to_all | solution.py:47
  529.1 5.1 copy-start.4
  529.1 7.3 copy-start.3
  531.7 68.6 %collective-permute-start = (f32[40,150,128]{2,0,1:T(8,128)S(1)}, f32[40,150,128]{2,0,1:T(8,128)S(1)}, u32[]{:S(2)}, u32[]{:S(2)}) collective-permute-start(f32[40,150,128]{2,0,1:T(8,128)S(1)} %copy.77), channel_id=1, source_target_pairs={{0,4},{4,0},{8,12},{12,8},{16,20},{20,16},{24,28},{28,24},{1,5},{5... | collective-permute-start | bytes 9216008 | tf_op jit(solution)/shard_map/ppermute | solution.py:23
  534.1 4.4 copy-start.2
  534.7 196.3 %collective-permute-start.1 = (f32[40,150,128]{2,0,1:T(8,128)S(1)}, f32[40,150,128]{2,0,1:T(8,128)S(1)}, u32[]{:S(2)}, u32[]{:S(2)}) collective-permute-start(f32[40,150,128]{2,0,1:T(8,128)S(1)} %copy.79), channel_id=1, source_target_pairs={{0,8},{4,12},{8,0},{12,4},{16,24},{20,28},{24,16},{28,20},{1,9},{5... | collective-permute-start | bytes 9216008 | tf_op jit(solution)/shard_map/ppermute | solution.py:23
  536.4 7.4 copy-start.1
  538.5 391.4 %collective-permute-start.2 = (f32[40,150,128]{2,0,1:T(8,128)}, f32[40,150,128]{2,0,1:T(8,128)}, u32[]{:S(2)}, u32[]{:S(2)}) collective-permute-start(f32[40,150,128]{2,0,1:T(8,128)} %copy.81), channel_id=1, source_target_pairs={{0,12},{4,8},{8,4},{12,0},{16,28},{20,24},{24,20},{28,16},{1,13},{... | collective-permute-start | bytes 9216008 | tf_op jit(solution)/shard_map/ppermute | solution.py:23
  538.5 8.7 copy-start
  540.8 455.8 %collective-permute-start.3 = (f32[40,150,128]{2,0,1:T(8,128)}, f32[40,150,128]{2,0,1:T(8,128)}, u32[]{:S(2)}, u32[]{:S(2)}) collective-permute-start(f32[40,150,128]{2,0,1:T(8,128)} %copy.83), channel_id=1, source_target_pairs={{0,16},{4,20},{8,24},{12,28},{16,0},{20,4},{24,8},{28,12},{1,17},{... | collective-permute-start | bytes 9216008 | tf_op jit(solution)/shard_map/ppermute | solution.py:23
  546.0 517.1 %collective-permute-start.4 = (f32[40,150,128]{2,0,1:T(8,128)}, f32[40,150,128]{2,0,1:T(8,128)}, u32[]{:S(2)}, u32[]{:S(2)}) collective-permute-start(f32[40,150,128]{2,0,1:T(8,128)} %copy.85), channel_id=1, source_target_pairs={{0,20},{4,16},{8,28},{12,24},{16,4},{20,0},{24,12},{28,8},{1,21},{... | collective-permute-start | bytes 9216008 | tf_op jit(solution)/shard_map/ppermute | solution.py:23
  600.3 130.6 %copy-start.5 = (f32[40,150,128]{2,0,1:T(8,128)}, f32[40,150,128]{2,0,1:T(8,128)S(1)}, u32[]{:S(2)}) copy-start(f32[40,150,128]{2,0,1:T(8,128)S(1)} %collective-permute-done) | copy-start | bytes 9216004
  600.3 529.2 %collective-permute-start.5 = (f32[40,150,128]{2,0,1:T(8,128)}, f32[40,150,128]{2,0,1:T(8,128)}, u32[]{:S(2)}, u32[]{:S(2)}) collective-permute-start(f32[40,150,128]{2,0,1:T(8,128)} %copy.87), channel_id=1, source_target_pairs={{0,24},{4,28},{8,16},{12,20},{16,8},{20,12},{24,0},{28,4},{1,25},{... | collective-permute-start | bytes 9216008 | tf_op jit(solution)/shard_map/ppermute | solution.py:23
  731.0 1.7 copy-start.7
  732.6 463.4 %collective-permute-start.6 = (f32[40,150,128]{2,0,1:T(8,128)}, f32[40,150,128]{2,0,1:T(8,128)}, u32[]{:S(2)}, u32[]{:S(2)}) collective-permute-start(f32[40,150,128]{2,0,1:T(8,128)} %copy.89), channel_id=1, source_target_pairs={{0,28},{4,24},{8,20},{12,16},{16,12},{20,8},{24,4},{28,0},{1,29},{... | collective-permute-start | bytes 9216008 | tf_op jit(solution)/shard_map/ppermute | solution.py:23
  753.7 43.1 %copy-start.6 = (f32[40,150,128]{2,0,1:T(8,128)S(1)}, f32[40,150,128]{2,0,1:T(8,128)}, u32[]{:S(2)}) copy-start(f32[40,150,128]{2,0,1:T(8,128)} %copy-done.5) | copy-start | bytes 9216004
  806.6 56.8 %copy-start.8 = (f32[40,150,128]{2,0,1:T(8,128)S(1)}, f32[40,150,128]{2,0,1:T(8,128)}, u32[]{:S(2)}) copy-start(f32[40,150,128]{2,0,1:T(8,128)} %copy-done.7) | copy-start | bytes 9216004
  1261.0 9.3 copy-start.9
  1261.0 332.8 %all-to-all-start.1 = ((f32[320,150,128]{0,1,2:T(8,128)}), f32[320,150,128]{0,1,2:T(8,128)}, u32[]{:S(2)}, u32[]{:S(2)}) async-start(f32[320,150,128]{0,1,2:T(8,128)} %dynamic_update_slice.31), calls=%async_computation.1 | async-start | bytes 59768832 | tf_op jit(solution)/shard_map/all_to_all | solution.py:52
